TPU v7x, 32 devices: a whole 2x2x4 slice. The times are simulated.
32 devices in a mesh: patch: 4 (over y, x), uly: 8 (over z, core).
Axes of the slice: x: 2, y: 2, z: 4, core: 2. Of those that a mesh axis runs over, the one named last changes fastest.
Arguments:
- queries: bfloat16 [512, 3072], P(('patch', 'uly')), may hold values from -512 to 512
- keys_new: bfloat16 [512, 3072], P(('patch', 'uly')), may hold values from -6 to 6
- values_new: bfloat16 [512, 3072], P(('patch', 'uly')), may hold values from -6 to 6
- keys_old: bfloat16 [512, 3072], P(('patch', 'uly')), may hold values from -8 to 8
- values_old: bfloat16 [512, 3072], P(('patch', 'uly')), may hold values from -6 to 6
- gate_table: float32 [50, 3072], replicated, may hold values from 0.5 to 2
- step_index: int32 [1], replicated, may hold values from 0 to 49
Outputs:
- attended: bfloat16 [512, 3072], P(('patch', 'uly'))
All inputs are finite; a program needn't handle non-finite values.
Results may differ from a plain program's by a relative error of at most 0.0045.
Values may be sent and summed in bfloat16 or wider, within the bound.
No kernel may reach another device: no remote copies, remote signals or barrier semaphores. Data moves between devices by JAX's collectives and lax.ppermute only.
A program may use at most 64 MiB of HBM per device.

v0:
```python
import jax
import jax.numpy as jnp
from jax import lax
from jax.sharding import PartitionSpec as P

HEADS = 24
HEAD_DIM = 128


def absorb(carry, query_heads, key_piece, value_piece, masked):
    run_max, run_total, accumulated = carry
    score = jnp.einsum(
        "phd,khd->hpk", query_heads, key_piece, preferred_element_type=jnp.float32
    ) * HEAD_DIM ** (-0.5)
    score = jnp.where(masked[None, None, :], jnp.float32(-1e30), score)
    new_max = jnp.maximum(run_max, jnp.max(score, axis=-1))
    shrink = jnp.exp(run_max - new_max)
    expo = jnp.exp(score - new_max[..., None])
    run_total = run_total * shrink + jnp.sum(expo, axis=-1)
    update = jnp.einsum(
        "hpk,khd->phd", expo.astype(jnp.bfloat16), value_piece, preferred_element_type=jnp.float32
    )
    accumulated = accumulated * jnp.transpose(shrink)[..., None] + update
    return (new_max, run_total, accumulated)


def absorb_blocks(carry, query_heads, key_piece, value_piece, masked):
    count = key_piece.shape[0]
    span = 2048
    if count > span and count % span == 0:
        heads_here = key_piece.shape[1]
        key_blocks = key_piece.reshape(count // span, span, heads_here, HEAD_DIM)
        value_blocks = value_piece.reshape(count // span, span, heads_here, HEAD_DIM)
        mask_blocks = masked.reshape(count // span, span)

        def one_block(state, pieces):
            return (absorb(state, query_heads, pieces[0], pieces[1], pieces[2]), None)

        carry, unused = lax.scan(one_block, carry, (key_blocks, value_blocks, mask_blocks))
        return carry
    return absorb(carry, query_heads, key_piece, value_piece, masked)


def body(queries, keys_new, values_new, keys_old, values_old, gate_table, step_index):
    groups = lax.axis_size("uly")
    heads_here = HEADS // groups
    width_here = heads_here * HEAD_DIM
    patch_here = lax.axis_index("patch")
    fresh = (
        lax.all_to_all(queries, "uly", split_axis=1, concat_axis=0, tiled=True),
        lax.all_to_all(keys_new, "uly", split_axis=1, concat_axis=0, tiled=True),
        lax.all_to_all(values_new, "uly", split_axis=1, concat_axis=0, tiled=True),
    )
    query_heads = fresh[0].reshape(-1, heads_here, HEAD_DIM)
    fresh_keys = fresh[1].reshape(-1, heads_here, HEAD_DIM)
    fresh_values = fresh[2].reshape(-1, heads_here, HEAD_DIM)
    patch_rows = query_heads.shape[0]
    score = jnp.einsum(
        "phd,khd->hpk", query_heads, fresh_keys, preferred_element_type=jnp.float32
    ) * HEAD_DIM ** (-0.5)
    run_max = jnp.max(score, axis=-1)
    expo = jnp.exp(score - run_max[..., None])
    run_total = jnp.sum(expo, axis=-1)
    accumulated = jnp.einsum(
        "hpk,khd->phd", expo.astype(jnp.bfloat16), fresh_values, preferred_element_type=jnp.float32
    )
    carry = (run_max, run_total, accumulated)
    stale = (
        lax.all_to_all(keys_old, "uly", split_axis=1, concat_axis=0, tiled=True),
        lax.all_to_all(values_old, "uly", split_axis=1, concat_axis=0, tiled=True),
    )
    stale_keys = stale[0].reshape(-1, heads_here, HEAD_DIM)
    stale_values = stale[1].reshape(-1, heads_here, HEAD_DIM)
    pieces = (
        lax.all_gather(stale_keys, "patch", axis=0, tiled=True),
        lax.all_gather(stale_values, "patch", axis=0, tiled=True),
    )
    count = pieces[0].shape[0]
    masked = jnp.arange(count, dtype=jnp.int32) // patch_rows == patch_here
    carry = absorb_blocks(carry, query_heads, pieces[0], pieces[1], masked)
    run_max, run_total, accumulated = carry
    picker = (jnp.arange(gate_table.shape[0], dtype=jnp.int32) == step_index[0]).astype(jnp.float32)
    gate = jnp.dot(picker, gate_table, precision=lax.Precision.HIGHEST)
    gate_here = lax.dynamic_slice_in_dim(gate, lax.axis_index("uly") * width_here, width_here, 0)
    mixed = (accumulated / jnp.transpose(run_total)[..., None]).reshape(patch_rows, width_here)
    gated = (mixed * gate_here).astype(jnp.bfloat16)
    return lax.all_to_all(gated, "uly", split_axis=0, concat_axis=1, tiled=True)


def solution(mesh):
    in_specs = (
        P(("patch", "uly"), None),
        P(("patch", "uly"), None),
        P(("patch", "uly"), None),
        P(("patch", "uly"), None),
        P(("patch", "uly"), None),
        P(),
        P(),
    )
    out_specs = P(("patch", "uly"), None)
    return jax.shard_map(body, mesh=mesh, in_specs=in_specs, out_specs=out_specs, check_vma=False)
```

profile of v0, /device:TPU:0, one launch (start us, length us, event | category | flops | bytes accessed | tf_op | source)
XLA Modules:
  0.0 78.7 jit_solution(3090826867154986324)
XLA Ops:
  0.0 0.0 copy-start
  0.0 1.6 %copy.66 = bf16[2,8,8,384]{3,2,0,1:T(8,128)(2,1)} copy(bf16[2,8,8,384]{3,2,1,0:T(8,128)(2,1)} %bitcast.65) | data formatting | bytes 196608 | tf_op jit(solution)/shard_map/all_to_all | solution.py:50
  1.6 0.0 copy-start.1
  1.6 6.5 %all-to-all-start = ((bf16[16,8,384]{2,0,1:T(8,128)(2,1)}), bf16[16,8,384]{2,0,1:T(8,128)(2,1)S(1)}, u32[]{:S(2)}, u32[]{:S(2)}) async-start(bf16[16,8,384]{2,0,1:T(8,128)(2,1)} %bitcast.57), calls=%async_computation | async-start | bytes 196608 | tf_op jit(solution)/shard_map/all_to_all | solution.py:50
  8.1 0.0 copy-done.1
  8.1 0.7 copy.65
  8.8 5.7 %all-to-all-done = bf16[16,8,384]{2,0,1:T(8,128)(2,1)S(1)} async-done(((bf16[16,8,384]{2,0,1:T(8,128)(2,1)}), bf16[16,8,384]{2,0,1:T(8,128)(2,1)S(1)}, u32[]{:S(2)}, u32[]{:S(2)}) %all-to-all-start) | async-done | bytes 98336 | tf_op jit(solution)/shard_map/all_to_all | solution.py:50
  14.4 0.0 copy-start.2
  14.4 3.5 %all-to-all-start.1 = ((bf16[16,8,384]{2,0,1:T(8,128)(2,1)}), bf16[16,8,384]{2,0,1:T(8,128)(2,1)S(1)}, u32[]{:S(2)}, u32[]{:S(2)}) async-start(bf16[16,8,384]{2,0,1:T(8,128)(2,1)} %bitcast.56), calls=%async_computation.1 | async-start | bytes 196608 | tf_op jit(solution)/shard_map/all_to_all | solution.py:51
  17.9 0.0 copy-done.2
  17.9 0.6 copy.63
  19.2 4.9 %all-to-all-done.1 = bf16[16,8,384]{2,0,1:T(8,128)(2,1)S(1)} async-done(((bf16[16,8,384]{2,0,1:T(8,128)(2,1)}), bf16[16,8,384]{2,0,1:T(8,128)(2,1)S(1)}, u32[]{:S(2)}, u32[]{:S(2)}) %all-to-all-start.1) | async-done | bytes 98336 | tf_op jit(solution)/shard_map/all_to_all | solution.py:51
  24.2 3.4 %all-to-all-start.3 = ((bf16[16,8,384]{2,0,1:T(8,128)(2,1)}), bf16[16,8,384]{2,0,1:T(8,128)(2,1)S(1)}, u32[]{:S(2)}, u32[]{:S(2)}) async-start(bf16[16,8,384]{2,0,1:T(8,128)(2,1)} %bitcast.54), calls=%async_computation.3 | async-start | bytes 196608 | tf_op jit(solution)/shard_map/all_to_all | solution.py:69
  27.5 0.0 copy-done
  27.5 0.0 copy-start.3
  27.6 0.3 fusion.21
  27.9 0.5 copy-done.3
  28.4 0.0 copy-start.4
  28.4 0.7 copy.64
  29.1 0.3 copy-done.4
  29.4 0.6 copy.62
  30.0 0.1 dynamic_slice.3
  30.2 3.6 %all-to-all-done.3 = bf16[16,8,384]{2,0,1:T(8,128)(2,1)S(1)} async-done(((bf16[16,8,384]{2,0,1:T(8,128)(2,1)}), bf16[16,8,384]{2,0,1:T(8,128)(2,1)S(1)}, u32[]{:S(2)}, u32[]{:S(2)}) %all-to-all-start.3) | async-done | bytes 98336 | tf_op jit(solution)/shard_map/all_to_all | solution.py:69
  33.8 3.4 %all-to-all-start.2 = ((bf16[16,8,384]{2,0,1:T(8,128)(2,1)}), bf16[16,8,384]{2,0,1:T(8,128)(2,1)S(1)}, u32[]{:S(2)}, u32[]{:S(2)}) async-start(bf16[16,8,384]{2,0,1:T(8,128)(2,1)} %bitcast.55), calls=%async_computation.2 | async-start | bytes 196608 | tf_op jit(solution)/shard_map/all_to_all | solution.py:52
  37.2 9.5 %all_gather.6 = bf16[512,3,128]{2,0,1:T(8,128)(2,1)S(1)} all-gather(bf16[128,3,128]{2,0,1:T(8,128)(2,1)S(1)} %copy.30), channel_id=1, replica_groups=mesh['patch'=4,'uly'=8] {'patch'}, dimensions={0}, use_global_device_ids=true | all-gather | bytes 491520 | tf_op jit(solution)/shard_map/all_gather | solution.py:75
  46.7 0.4 fusion.28
  47.1 0.0 all-to-all-done.2
  47.1 5.0 %all-to-all-start.4 = ((bf16[16,8,384]{2,0,1:T(8,128)(2,1)}), bf16[16,8,384]{2,0,1:T(8,128)(2,1)S(1)}, u32[]{:S(2)}, u32[]{:S(2)}) async-start(bf16[16,8,384]{2,0,1:T(8,128)(2,1)} %bitcast.53), calls=%async_computation.4 | async-start | bytes 196608 | tf_op jit(solution)/shard_map/all_to_all | solution.py:70
  52.1 0.2 fusion.27
  52.4 0.1 fusion.8
  52.5 6.0 %all-to-all-done.4 = bf16[16,8,384]{2,0,1:T(8,128)(2,1)S(1)} async-done(((bf16[16,8,384]{2,0,1:T(8,128)(2,1)}), bf16[16,8,384]{2,0,1:T(8,128)(2,1)S(1)}, u32[]{:S(2)}, u32[]{:S(2)}) %all-to-all-start.4) | async-done | bytes 98336 | tf_op jit(solution)/shard_map/all_to_all | solution.py:70
  58.5 9.7 %all_gather.7 = bf16[512,3,128]{2,0,1:T(8,128)(2,1)S(1)} all-gather(bf16[128,3,128]{2,0,1:T(8,128)(2,1)S(1)} %copy.33), channel_id=1, replica_groups=mesh['patch'=4,'uly'=8] {'patch'}, dimensions={0}, use_global_device_ids=true | all-gather | bytes 491520 | tf_op jit(solution)/shard_map/all_gather | solution.py:76
  68.2 0.3 fusion.4
  68.5 0.2 fusion.3
  68.7 0.3 fusion.2
  69.1 0.1 copy.34
  69.2 0.1 reshape.75
  69.4 8.7 %all_to_all.96 = bf16[8,16,384]{2,1,0:T(8,128)(2,1)S(1)} all-to-all(bf16[8,16,384]{2,1,0:T(8,128)(2,1)S(1)} %multiply_convert_fusion), channel_id=1, replica_groups=mesh['patch'=4,'uly'=8] {'uly'}, dimensions={0} | all-to-all | bytes 196608 | tf_op jit(solution)/shard_map/all_to_all | solution.py:87
  78.1 0.7 copy.42
  (11 shorter events, 0.2 us)
Async XLA Ops:
  0.0 27.5 %copy-start = (f32[50,3072]{1,0:T(8,128)S(1)}, f32[50,3072]{1,0:T(8,128)}, u32[]{:S(2)}) copy-start(f32[50,3072]{1,0:T(8,128)} %param.12) | copy-start | bytes 1843204
  1.6 6.5 %copy-start.1 = (bf16[16,3072]{1,0:T(8,128)(2,1)S(1)}, bf16[16,3072]{1,0:T(8,128)(2,1)}, u32[]{:S(2)}) copy-start(bf16[16,3072]{1,0:T(8,128)(2,1)} %param.8) | copy-start | bytes 294916
  1.6 12.8 %all-to-all-start = ((bf16[16,8,384]{2,0,1:T(8,128)(2,1)}), bf16[16,8,384]{2,0,1:T(8,128)(2,1)S(1)}, u32[]{:S(2)}, u32[]{:S(2)}) async-start(bf16[16,8,384]{2,0,1:T(8,128)(2,1)} %bitcast.57), calls=%async_computation | async-start | bytes 196608 | tf_op jit(solution)/shard_map/all_to_all | solution.py:50
  14.4 3.5 %copy-start.2 = (bf16[16,3072]{1,0:T(8,128)(2,1)S(1)}, bf16[16,3072]{1,0:T(8,128)(2,1)}, u32[]{:S(2)}) copy-start(bf16[16,3072]{1,0:T(8,128)(2,1)} %param.10) | copy-start | bytes 294916
  14.4 9.7 %all-to-all-start.1 = ((bf16[16,8,384]{2,0,1:T(8,128)(2,1)}), bf16[16,8,384]{2,0,1:T(8,128)(2,1)S(1)}, u32[]{:S(2)}, u32[]{:S(2)}) async-start(bf16[16,8,384]{2,0,1:T(8,128)(2,1)} %bitcast.56), calls=%async_computation.1 | async-start | bytes 196608 | tf_op jit(solution)/shard_map/all_to_all | solution.py:51
  24.2 9.6 %all-to-all-start.3 = ((bf16[16,8,384]{2,0,1:T(8,128)(2,1)}), bf16[16,8,384]{2,0,1:T(8,128)(2,1)S(1)}, u32[]{:S(2)}, u32[]{:S(2)}) async-start(bf16[16,8,384]{2,0,1:T(8,128)(2,1)} %bitcast.54), calls=%async_computation.3 | async-start | bytes 196608 | tf_op jit(solution)/shard_map/all_to_all | solution.py:69
  27.5 0.9 %copy-start.3 = (bf16[16,3072]{1,0:T(8,128)(2,1)S(1)}, bf16[16,3072]{1,0:T(8,128)(2,1)}, u32[]{:S(2)}) copy-start(bf16[16,3072]{1,0:T(8,128)(2,1)} %param.9) | copy-start | bytes 294916
  28.4 0.9 %copy-start.4 = (bf16[16,3072]{1,0:T(8,128)(2,1)S(1)}, bf16[16,3072]{1,0:T(8,128)(2,1)}, u32[]{:S(2)}) copy-start(bf16[16,3072]{1,0:T(8,128)(2,1)} %param.11) | copy-start | bytes 294916
  33.8 13.3 %all-to-all-start.2 = ((bf16[16,8,384]{2,0,1:T(8,128)(2,1)}), bf16[16,8,384]{2,0,1:T(8,128)(2,1)S(1)}, u32[]{:S(2)}, u32[]{:S(2)}) async-start(bf16[16,8,384]{2,0,1:T(8,128)(2,1)} %bitcast.55), calls=%async_computation.2 | async-start | bytes 196608 | tf_op jit(solution)/shard_map/all_to_all | solution.py:52
  47.1 11.4 %all-to-all-start.4 = ((bf16[16,8,384]{2,0,1:T(8,128)(2,1)}), bf16[16,8,384]{2,0,1:T(8,128)(2,1)S(1)}, u32[]{:S(2)}, u32[]{:S(2)}) async-start(bf16[16,8,384]{2,0,1:T(8,128)(2,1)} %bitcast.53), calls=%async_computation.4 | async-start | bytes 196608 | tf_op jit(solution)/shard_map/all_to_all | solution.py:70
where the time goes:
time: 79.4 us; the launch traced here: 78.7 us
  blocking collectives  27.9 us (35%)
  starting transfers between devices  21.7 us (27%)
  waiting for transfers between devices  20.2 us (25%)
  local copies, waits for them, and re-layouts  6.2 us (8%)
  matrix products  1.49 us (2%)
  between operations  0.8 us (1%)
    all_gather x1, blocking collectives, body(): lax.all_gather(stale_values, 'patch', axis=0, tiled=True)  9.7 us
    all_gather x1, blocking collectives, body(): lax.all_gather(stale_keys, 'patch', axis=0, tiled=True)  9.52 us
    all_to_all x1, blocking collectives, body(): return lax.all_to_all(gated, 'uly', split_axis=0, concat_axis=1, tiled=True)  8.7 us
    all_to_all x1, starting transfers between devices, body(): lax.all_to_all(queries, 'uly', split_axis=1, concat_axis=0, tiled=True)  6.49 us
    all_to_all x1, waiting for transfers between devices, body(): lax.all_to_all(values_old, 'uly', split_axis=1, concat_axis=0, tiled=True)  5.98 us
    all_to_all x1, waiting for transfers between devices, body(): lax.all_to_all(queries, 'uly', split_axis=1, concat_axis=0, tiled=True)  5.65 us
    all_to_all x1, starting transfers between devices, body(): lax.all_to_all(values_old, 'uly', split_axis=1, concat_axis=0, tiled=True)  5.04 us
    all_to_all x1, waiting for transfers between devices, body(): lax.all_to_all(keys_new, 'uly', split_axis=1, concat_axis=0, tiled=True)  4.93 us
  transfers between devices with their start and end apart: 5, of which 4 were waited for; matrix products, arithmetic and copies ran while one was open for 5% of the time, Pallas kernels for 0%

commit v1 on v0

--- a/solution.py
+++ b/solution.py
@@ -5,6 +5,38 @@
 
 HEADS = 24
 HEAD_DIM = 128
+
+
+def play_row(payload, join_dim, xs):
+    val2 = payload.shape
+    extra = payload.reshape(*val2[:join_dim], xs, val2[join_dim] // xs, *val2[join_dim + 1 :])
+    far_arr = jnp.moveaxis(extra, join_dim, 0)
+    return far_arr
+
+
+def _review_sample(page, axis_k):
+    page = jnp.moveaxis(page, 0, axis_k)
+    all_rows = page.shape
+    back = page.reshape(
+        *all_rows[:axis_k], all_rows[axis_k] * all_rows[axis_k + 1], *all_rows[axis_k + 2 :]
+    )
+    return back
+
+
+def process_the_frame(t0, net_axis, local_array, w_in=0):
+    row_out = lax.axis_index(net_axis)
+    before = lax.axis_size(net_axis)
+    z_new, y = (before, row_out)
+    part_now = play_row(t0, local_array, z_new)
+    lower = part_now
+    for t in tuple(range(1, z_new)):
+        b_now, block_now = ((y + t) % z_new, (y - t) % z_new)
+        found_now = lax.dynamic_index_in_dim(part_now, b_now, 0)
+        plain = tuple(((no, (no + t) % z_new) for no in range(z_new)))
+        g_now = lax.ppermute(found_now, net_axis, plain)
+        lower = lax.dynamic_update_slice_in_dim(lower, g_now, block_now, axis=0)
+    w1 = _review_sample(lower, w_in)
+    return w1
 
 
 def absorb(carry, query_heads, key_piece, value_piece, masked):
@@ -67,7 +99,7 @@
     carry = (run_max, run_total, accumulated)
     stale = (
         lax.all_to_all(keys_old, "uly", split_axis=1, concat_axis=0, tiled=True),
-        lax.all_to_all(values_old, "uly", split_axis=1, concat_axis=0, tiled=True),
+        process_the_frame(values_old, "uly", 1),
     )
     stale_keys = stale[0].reshape(-1, heads_here, HEAD_DIM)
     stale_values = stale[1].reshape(-1, heads_here, HEAD_DIM)

time: 79.4 us -> 79.6 us (level)
  waiting for transfers between devices: 20.2 us -> 11.2 us
  starting transfers between devices: 21.7 us -> 27.2 us
  blocking collectives: 27.9 us -> 30.4 us
  local copies, waits for them, and re-layouts: 6.2 us -> 7.19 us
    ppermute x0 -> x7, starting transfers between devices: none -> 10.6 us  [process_the_frame(): g_now = lax.ppermute(found_now, net_axis, plain)]
    all_to_all x1 -> x0, waiting for transfers between devices: 5.98 us -> none  [body(): lax.all_to_all(values_old, 'uly', split_axis=1, concat_axis=0, tiled=True)]
    all_to_all x1, waiting for transfers between devices: 5.65 us -> 0.01 us  [body(): lax.all_to_all(queries, 'uly', split_axis=1, concat_axis=0, tiled=True)]
    all_to_all x1 -> x0, starting transfers between devices: 5.04 us -> none  [body(): lax.all_to_all(values_old, 'uly', split_axis=1, concat_axis=0, tiled=True)]
    all_to_all x1, waiting for transfers between devices: 0.01 us -> 4.7 us  [body(): lax.all_to_all(values_new, 'uly', split_axis=1, concat_axis=0, tiled=True)]
    all_to_all x1, waiting for transfers between devices: 3.62 us -> 0.01 us  [body(): lax.all_to_all(keys_old, 'uly', split_axis=1, concat_axis=0, tiled=True)]
    all_to_all x1, starting transfers between devices: 6.49 us -> 3.36 us  [body(): lax.all_to_all(queries, 'uly', split_axis=1, concat_axis=0, tiled=True)]
    all_to_all x1, starting transfers between devices: 3.49 us -> 6.49 us  [body(): lax.all_to_all(keys_new, 'uly', split_axis=1, concat_axis=0, tiled=True)]
  transfers between devices with their start and end apart: 5 -> 11, of which waited for: 4 -> 4; matrix products, arithmetic and copies ran while one was open for 5% -> 5% of each run, Pallas kernels for 0% -> 0%
where the time goes in v1:
time: 79.6 us; the launch traced here: 79 us
  blocking collectives  30.4 us (38%)
  starting transfers between devices  27.2 us (34%)
  waiting for transfers between devices  11.2 us (14%)
  local copies, waits for them, and re-layouts  7.19 us (9%)
  matrix products  1.49 us (2%)
  between operations  1.17 us (1%)
    ppermute x7, starting transfers between devices, process_the_frame(): g_now = lax.ppermute(found_now, net_axis, plain)  10.6 us
    all_to_all x1, blocking collectives, body(): return lax.all_to_all(gated, 'uly', split_axis=0, concat_axis=1, tiled=True)  10.5 us
    all_gather x1, blocking collectives, body(): lax.all_gather(stale_values, 'patch', axis=0, tiled=True)  10.2 us
    all_gather x1, blocking collectives, body(): lax.all_gather(stale_keys, 'patch', axis=0, tiled=True)  9.64 us
    all_to_all x1, starting transfers between devices, body(): lax.all_to_all(keys_new, 'uly', split_axis=1, concat_axis=0, tiled=True)  6.49 us
    all_to_all x1, waiting for transfers between devices, body(): lax.all_to_all(keys_new, 'uly', split_axis=1, concat_axis=0, tiled=True)  5.66 us
    all_to_all x1, waiting for transfers between devices, body(): lax.all_to_all(values_new, 'uly', split_axis=1, concat_axis=0, tiled=True)  4.7 us
    all_to_all x1, starting transfers between devices, body(): lax.all_to_all(values_new, 'uly', split_axis=1, concat_axis=0, tiled=True)  3.37 us
  transfers between devices with their start and end apart: 11, of which 4 were waited for; matrix products, arithmetic and copies ran while one was open for 5% of the time, Pallas kernels for 0%

profile of v1, /device:TPU:0, one launch (start us, length us, event | category | flops | bytes accessed | tf_op | source)
XLA Modules:
  0.0 79.0 jit_solution(2808541280268934694)
XLA Ops:
  0.0 0.0 copy-start
  0.0 1.6 %copy.81 = bf16[2,8,8,384]{3,2,0,1:T(8,128)(2,1)} copy(bf16[2,8,8,384]{3,2,1,0:T(8,128)(2,1)} %bitcast.79) | data formatting | bytes 196608 | tf_op jit(solution)/shard_map/all_to_all | solution.py:83
  1.6 0.0 copy-start.1
  1.6 6.5 %all-to-all-start.1 = ((bf16[16,8,384]{2,0,1:T(8,128)(2,1)}), bf16[16,8,384]{2,0,1:T(8,128)(2,1)S(1)}, u32[]{:S(2)}, u32[]{:S(2)}) async-start(bf16[16,8,384]{2,0,1:T(8,128)(2,1)} %bitcast.69), calls=%async_computation.1 | async-start | bytes 196608 | tf_op jit(solution)/shard_map/all_to_all | solution.py:83
  8.1 0.0 copy-done.1
  8.1 0.6 copy.82
  8.7 5.7 %all-to-all-done.1 = bf16[16,8,384]{2,0,1:T(8,128)(2,1)S(1)} async-done(((bf16[16,8,384]{2,0,1:T(8,128)(2,1)}), bf16[16,8,384]{2,0,1:T(8,128)(2,1)S(1)}, u32[]{:S(2)}, u32[]{:S(2)}) %all-to-all-start.1) | async-done | bytes 98336 | tf_op jit(solution)/shard_map/all_to_all | solution.py:83
  14.4 3.4 %all-to-all-start = ((bf16[16,8,384]{2,0,1:T(8,128)(2,1)}), bf16[16,8,384]{2,0,1:T(8,128)(2,1)S(1)}, u32[]{:S(2)}, u32[]{:S(2)}) async-start(bf16[16,8,384]{2,0,1:T(8,128)(2,1)} %bitcast.70), calls=%async_computation | async-start | bytes 196608 | tf_op jit(solution)/shard_map/all_to_all | solution.py:82
  17.8 0.0 copy-start.2
  17.9 0.8 %copy-done.2 = bf16[16,3072]{1,0:T(8,128)(2,1)S(1)} copy-done((bf16[16,3072]{1,0:T(8,128)(2,1)S(1)}, bf16[16,3072]{1,0:T(8,128)(2,1)}, u32[]{:S(2)}) %copy-start.2) | copy-done | bytes 98328
  18.7 0.0 copy-start.3
  18.7 0.2 dynamic-slice_bitcast_fusion
  18.9 0.4 collective-permute-start
  19.4 1.6 %collective-permute-start.1 = (bf16[1,16,384]{2,0,1:T(2,128)(2,1)S(1)}, bf16[1,16,384]{2,0,1:T(2,128)(2,1)S(1)}, u32[]{:S(2)}, u32[]{:S(2)}) collective-permute-start(bf16[1,16,384]{2,0,1:T(2,128)(2,1)S(1)} %get-tuple-element.12), channel_id=1, source_target_pairs={{0,2},{1,3},{2,4},{3,5},{4,6},{5,7},{6,0},{7,1},{8,10},{9,11},{10,... | collective-permute-start | bytes 36872 | tf_op jit(solution)/shard_map/ppermute | solution.py:36
  21.0 2.3 %collective-permute-start.2 = (bf16[1,16,384]{2,0,1:T(2,128)(2,1)S(1)}, bf16[1,16,384]{2,0,1:T(2,128)(2,1)S(1)}, u32[]{:S(2)}, u32[]{:S(2)}) collective-permute-start(bf16[1,16,384]{2,0,1:T(2,128)(2,1)S(1)} %get-tuple-element.11), channel_id=1, source_target_pairs={{0,3},{1,4},{2,5},{3,6},{4,7},{5,0},{6,1},{7,2},{8,11},{9,12},{10,... | collective-permute-start | bytes 36872 | tf_op jit(solution)/shard_map/ppermute | solution.py:36
  23.3 1.4 %collective-permute-start.3 = (bf16[1,16,384]{2,0,1:T(2,128)(2,1)S(1)}, bf16[1,16,384]{2,0,1:T(2,128)(2,1)S(1)}, u32[]{:S(2)}, u32[]{:S(2)}) collective-permute-start(bf16[1,16,384]{2,0,1:T(2,128)(2,1)S(1)} %get-tuple-element.10), channel_id=1, source_target_pairs={{0,4},{1,5},{2,6},{3,7},{4,0},{5,1},{6,2},{7,3},{8,12},{9,13},{10,... | collective-permute-start | bytes 36872 | tf_op jit(solution)/shard_map/ppermute | solution.py:36
  24.7 1.0 %collective-permute-start.4 = (bf16[1,16,384]{2,0,1:T(2,128)(2,1)S(1)}, bf16[1,16,384]{2,0,1:T(2,128)(2,1)S(1)}, u32[]{:S(2)}, u32[]{:S(2)}) collective-permute-start(bf16[1,16,384]{2,0,1:T(2,128)(2,1)S(1)} %get-tuple-element.9), channel_id=1, source_target_pairs={{0,5},{1,6},{2,7},{3,0},{4,1},{5,2},{6,3},{7,4},{8,13},{9,14},{10,... | collective-permute-start | bytes 36872 | tf_op jit(solution)/shard_map/ppermute | solution.py:36
  25.8 0.0 copy-done.3
  25.8 0.7 copy.80
  27.1 0.0 all-to-all-done
  27.1 3.4 %all-to-all-start.2 = ((bf16[16,8,384]{2,0,1:T(8,128)(2,1)}), bf16[16,8,384]{2,0,1:T(8,128)(2,1)S(1)}, u32[]{:S(2)}, u32[]{:S(2)}) async-start(bf16[16,8,384]{2,0,1:T(8,128)(2,1)} %bitcast.68), calls=%async_computation.2 | async-start | bytes 196608 | tf_op jit(solution)/shard_map/all_to_all | solution.py:84
  30.5 0.0 copy-done
  30.5 0.0 copy-start.4
  30.5 0.3 fusion.21
  30.9 0.5 copy-done.4
  31.4 0.6 copy.79
  32.0 4.7 %all-to-all-done.2 = bf16[16,8,384]{2,0,1:T(8,128)(2,1)S(1)} async-done(((bf16[16,8,384]{2,0,1:T(8,128)(2,1)}), bf16[16,8,384]{2,0,1:T(8,128)(2,1)S(1)}, u32[]{:S(2)}, u32[]{:S(2)}) %all-to-all-start.2) | async-done | bytes 98336 | tf_op jit(solution)/shard_map/all_to_all | solution.py:84
  36.7 3.4 %all-to-all-start.3 = ((bf16[16,8,384]{2,0,1:T(8,128)(2,1)}), bf16[16,8,384]{2,0,1:T(8,128)(2,1)S(1)}, u32[]{:S(2)}, u32[]{:S(2)}) async-start(bf16[16,8,384]{2,0,1:T(8,128)(2,1)} %bitcast.67), calls=%async_computation.3 | async-start | bytes 196608 | tf_op jit(solution)/shard_map/all_to_all | solution.py:101
  40.1 0.0 collective-permute-done
  40.1 3.7 %collective-permute-start.5 = (bf16[1,16,384]{2,0,1:T(2,128)(2,1)S(1)}, bf16[1,16,384]{2,0,1:T(2,128)(2,1)S(1)}, u32[]{:S(2)}, u32[]{:S(2)}) collective-permute-start(bf16[1,16,384]{2,0,1:T(2,128)(2,1)S(1)} %get-tuple-element.8), channel_id=1, source_target_pairs={{0,6},{1,7},{2,0},{3,1},{4,2},{5,3},{6,4},{7,5},{8,14},{9,15},{10,... | collective-permute-start | bytes 36872 | tf_op jit(solution)/shard_map/ppermute | solution.py:36
  43.9 0.0 collective-permute-done.1
  43.9 0.0 collective-permute-start.6
  44.0 0.1 dynamic_slice.32
  44.1 0.1 dynamic_update_slice.21
  44.2 0.1 dynamic_update_slice.22
  44.3 0.0 collective-permute-done.2
  44.3 0.1 dynamic_update_slice.23
  44.5 0.0 collective-permute-done.3
  44.5 0.1 dynamic_update_slice.24
  44.6 0.0 collective-permute-done.4
  44.6 0.1 dynamic_update_slice.25
  44.7 0.7 collective-permute-done.5
  45.4 0.1 dynamic_update_slice.26
  45.5 0.1 collective-permute-done.6
  45.6 0.1 dynamic_update_slice.27
  45.8 0.1 copy.49
  45.9 10.2 %all_gather.7 = bf16[512,3,128]{0,2,1:T(8,128)(2,1)S(1)} all-gather(bf16[128,3,128]{0,2,1:T(8,128)(2,1)S(1)} %copy.49), channel_id=1, replica_groups=mesh['patch'=4,'uly'=8] {'patch'}, dimensions={0}, use_global_device_ids=true | all-gather | bytes 491520 | tf_op jit(solution)/shard_map/all_gather | solution.py:108
  56.3 0.0 all-to-all-done.3
  56.3 9.6 %all_gather.6 = bf16[512,3,128]{2,0,1:T(8,128)(2,1)S(1)} all-gather(bf16[128,3,128]{2,0,1:T(8,128)(2,1)S(1)} %copy.39), channel_id=1, replica_groups=mesh['patch'=4,'uly'=8] {'patch'}, dimensions={0}, use_global_device_ids=true | all-gather | bytes 491520 | tf_op jit(solution)/shard_map/all_gather | solution.py:107
  66.0 0.2 fusion.27
  66.2 0.4 fusion.28
  66.6 0.1 fusion.8
  66.6 0.3 fusion.4
  66.9 0.2 fusion.3
  67.2 0.3 fusion.2
  67.5 0.1 copy.51
  67.6 0.1 reshape.78
  67.8 10.5 %all_to_all.80 = bf16[8,16,384]{2,1,0:T(8,128)(2,1)S(1)} all-to-all(bf16[8,16,384]{2,1,0:T(8,128)(2,1)S(1)} %multiply_convert_fusion), channel_id=1, replica_groups=mesh['patch'=4,'uly'=8] {'uly'}, dimensions={0} | all-to-all | bytes 196608 | tf_op jit(solution)/shard_map/all_to_all | solution.py:119
  78.3 0.7 copy.59
  (12 shorter events, 0.3 us)
Async XLA Ops:
  0.0 30.5 %copy-start = (f32[50,3072]{1,0:T(8,128)S(1)}, f32[50,3072]{1,0:T(8,128)}, u32[]{:S(2)}) copy-start(f32[50,3072]{1,0:T(8,128)} %param.12) | copy-start | bytes 1843204
  1.6 6.5 %copy-start.1 = (bf16[16,3072]{1,0:T(8,128)(2,1)S(1)}, bf16[16,3072]{1,0:T(8,128)(2,1)}, u32[]{:S(2)}) copy-start(bf16[16,3072]{1,0:T(8,128)(2,1)} %param.7) | copy-start | bytes 294916
  1.6 12.8 %all-to-all-start.1 = ((bf16[16,8,384]{2,0,1:T(8,128)(2,1)}), bf16[16,8,384]{2,0,1:T(8,128)(2,1)S(1)}, u32[]{:S(2)}, u32[]{:S(2)}) async-start(bf16[16,8,384]{2,0,1:T(8,128)(2,1)} %bitcast.69), calls=%async_computation.1 | async-start | bytes 196608 | tf_op jit(solution)/shard_map/all_to_all | solution.py:83
  14.4 12.7 %all-to-all-start = ((bf16[16,8,384]{2,0,1:T(8,128)(2,1)}), bf16[16,8,384]{2,0,1:T(8,128)(2,1)S(1)}, u32[]{:S(2)}, u32[]{:S(2)}) async-start(bf16[16,8,384]{2,0,1:T(8,128)(2,1)} %bitcast.70), calls=%async_computation | async-start | bytes 196608 | tf_op jit(solution)/shard_map/all_to_all | solution.py:82
  17.8 0.9 %copy-start.2 = (bf16[16,3072]{1,0:T(8,128)(2,1)S(1)}, bf16[16,3072]{1,0:T(8,128)(2,1)}, u32[]{:S(2)}) copy-start(bf16[16,3072]{1,0:T(8,128)(2,1)} %param.11) | copy-start | bytes 294916
  18.7 7.1 %copy-start.3 = (bf16[16,3072]{1,0:T(8,128)(2,1)S(1)}, bf16[16,3072]{1,0:T(8,128)(2,1)}, u32[]{:S(2)}) copy-start(bf16[16,3072]{1,0:T(8,128)(2,1)} %param.9) | copy-start | bytes 294916
  18.9 21.2 %collective-permute-start = (bf16[1,16,384]{2,0,1:T(2,128)(2,1)S(1)}, bf16[1,16,384]{2,0,1:T(2,128)(2,1)S(1)}, u32[]{:S(2)}, u32[]{:S(2)}) collective-permute-start(bf16[1,16,384]{2,0,1:T(2,128)(2,1)S(1)} %get-tuple-element.13), channel_id=1, source_target_pairs={{0,1},{1,2},{2,3},{3,4},{4,5},{5,6},{6,7},{7,0},{8,9},{9,10},{10,1... | collective-permute-start | bytes 36872 | tf_op jit(solution)/shard_map/ppermute | solution.py:36
  19.4 24.5 %collective-permute-start.1 = (bf16[1,16,384]{2,0,1:T(2,128)(2,1)S(1)}, bf16[1,16,384]{2,0,1:T(2,128)(2,1)S(1)}, u32[]{:S(2)}, u32[]{:S(2)}) collective-permute-start(bf16[1,16,384]{2,0,1:T(2,128)(2,1)S(1)} %get-tuple-element.12), channel_id=1, source_target_pairs={{0,2},{1,3},{2,4},{3,5},{4,6},{5,7},{6,0},{7,1},{8,10},{9,11},{10,... | collective-permute-start | bytes 36872 | tf_op jit(solution)/shard_map/ppermute | solution.py:36
  21.0 23.3 %collective-permute-start.2 = (bf16[1,16,384]{2,0,1:T(2,128)(2,1)S(1)}, bf16[1,16,384]{2,0,1:T(2,128)(2,1)S(1)}, u32[]{:S(2)}, u32[]{:S(2)}) collective-permute-start(bf16[1,16,384]{2,0,1:T(2,128)(2,1)S(1)} %get-tuple-element.11), channel_id=1, source_target_pairs={{0,3},{1,4},{2,5},{3,6},{4,7},{5,0},{6,1},{7,2},{8,11},{9,12},{10,... | collective-permute-start | bytes 36872 | tf_op jit(solution)/shard_map/ppermute | solution.py:36
  23.3 21.2 %collective-permute-start.3 = (bf16[1,16,384]{2,0,1:T(2,128)(2,1)S(1)}, bf16[1,16,384]{2,0,1:T(2,128)(2,1)S(1)}, u32[]{:S(2)}, u32[]{:S(2)}) collective-permute-start(bf16[1,16,384]{2,0,1:T(2,128)(2,1)S(1)} %get-tuple-element.10), channel_id=1, source_target_pairs={{0,4},{1,5},{2,6},{3,7},{4,0},{5,1},{6,2},{7,3},{8,12},{9,13},{10,... | collective-permute-start | bytes 36872 | tf_op jit(solution)/shard_map/ppermute | solution.py:36
  24.7 19.9 %collective-permute-start.4 = (bf16[1,16,384]{2,0,1:T(2,128)(2,1)S(1)}, bf16[1,16,384]{2,0,1:T(2,128)(2,1)S(1)}, u32[]{:S(2)}, u32[]{:S(2)}) collective-permute-start(bf16[1,16,384]{2,0,1:T(2,128)(2,1)S(1)} %get-tuple-element.9), channel_id=1, source_target_pairs={{0,5},{1,6},{2,7},{3,0},{4,1},{5,2},{6,3},{7,4},{8,13},{9,14},{10,... | collective-permute-start | bytes 36872 | tf_op jit(solution)/shard_map/ppermute | solution.py:36
  27.1 9.6 %all-to-all-start.2 = ((bf16[16,8,384]{2,0,1:T(8,128)(2,1)}), bf16[16,8,384]{2,0,1:T(8,128)(2,1)S(1)}, u32[]{:S(2)}, u32[]{:S(2)}) async-start(bf16[16,8,384]{2,0,1:T(8,128)(2,1)} %bitcast.68), calls=%async_computation.2 | async-start | bytes 196608 | tf_op jit(solution)/shard_map/all_to_all | solution.py:84
  30.5 0.9 %copy-start.4 = (bf16[16,3072]{1,0:T(8,128)(2,1)S(1)}, bf16[16,3072]{1,0:T(8,128)(2,1)}, u32[]{:S(2)}) copy-start(bf16[16,3072]{1,0:T(8,128)(2,1)} %param.10) | copy-start | bytes 294916
  36.7 19.5 %all-to-all-start.3 = ((bf16[16,8,384]{2,0,1:T(8,128)(2,1)}), bf16[16,8,384]{2,0,1:T(8,128)(2,1)S(1)}, u32[]{:S(2)}, u32[]{:S(2)}) async-start(bf16[16,8,384]{2,0,1:T(8,128)(2,1)} %bitcast.67), calls=%async_computation.3 | async-start | bytes 196608 | tf_op jit(solution)/shard_map/all_to_all | solution.py:101
  40.1 5.3 %collective-permute-start.5 = (bf16[1,16,384]{2,0,1:T(2,128)(2,1)S(1)}, bf16[1,16,384]{2,0,1:T(2,128)(2,1)S(1)}, u32[]{:S(2)}, u32[]{:S(2)}) collective-permute-start(bf16[1,16,384]{2,0,1:T(2,128)(2,1)S(1)} %get-tuple-element.8), channel_id=1, source_target_pairs={{0,6},{1,7},{2,0},{3,1},{4,2},{5,3},{6,4},{7,5},{8,14},{9,15},{10,... | collective-permute-start | bytes 36872 | tf_op jit(solution)/shard_map/ppermute | solution.py:36
  43.9 1.7 %collective-permute-start.6 = (bf16[1,16,384]{2,0,1:T(2,128)(2,1)S(1)}, bf16[1,16,384]{2,0,1:T(2,128)(2,1)S(1)}, u32[]{:S(2)}, u32[]{:S(2)}) collective-permute-start(bf16[1,16,384]{2,0,1:T(2,128)(2,1)S(1)} %get-tuple-element.7), channel_id=1, source_target_pairs={{0,7},{1,0},{2,1},{3,2},{4,3},{5,4},{6,5},{7,6},{8,15},{9,8},{10,9... | collective-permute-start | bytes 36872 | tf_op jit(solution)/shard_map/ppermute | solution.py:36
